TPU v7x, 32 devices: a whole 2x2x4 slice. The times are simulated.
32 devices in a mesh: fsdp: 16 (over z, y, x), replica: 2 (over core).
Axes of the slice: x: 2, y: 2, z: 4, core: 2. Of those that a mesh axis runs over, the one named last changes fastest.
Arguments:
- inputs: bfloat16 [4096, 1024], P(('fsdp', 'replica')), may hold values from -6 to 6
- cotangent: bfloat16 [4096, 1024], P(('fsdp', 'replica')), may hold values from -6 to 6
- attn_gain: bfloat16 [1024], P('fsdp'), may hold values from 0.5 to 1.5
- attn_shift: bfloat16 [1024], P('fsdp'), may hold values from -3 to 3
- qkv_weight: bfloat16 [1024, 3072], P('fsdp'), as said below
- qkv_bias: bfloat16 [3072], P('fsdp'), may hold values from -3 to 3
- proj_weight: bfloat16 [1024, 1024], P('fsdp'), may hold values from -1 to 1
- proj_bias: bfloat16 [1024], P('fsdp'), may hold values from -3 to 3
- mlp_gain: bfloat16 [1024], P('fsdp'), may hold values from 0.5 to 1.5
- mlp_shift: bfloat16 [1024], P('fsdp'), may hold values from -3 to 3
- up_weight: bfloat16 [1024, 4096], P('fsdp'), may hold values from -0.1875 to 0.1875
- up_bias: bfloat16 [4096], P('fsdp'), may hold values from -3 to 3
- down_weight: bfloat16 [4096, 1024], P('fsdp'), may hold values from -0.09375 to 0.09375
- down_bias: bfloat16 [1024], P('fsdp'), may hold values from -3 to 3
Outputs:
- output: bfloat16 [4096, 1024], P(('fsdp', 'replica'))
- grad_inputs: bfloat16 [4096, 1024], P(('fsdp', 'replica'))
- grad_attn_gain: float32 [1024], P('fsdp')
- grad_attn_shift: float32 [1024], P('fsdp')
- grad_qkv_weight: float32 [1024, 3072], P('fsdp')
- grad_qkv_bias: float32 [3072], P('fsdp')
- grad_proj_weight: float32 [1024, 1024], P('fsdp')
- grad_proj_bias: float32 [1024], P('fsdp')
- grad_mlp_gain: float32 [1024], P('fsdp')
- grad_mlp_shift: float32 [1024], P('fsdp')
- grad_up_weight: float32 [1024, 4096], P('fsdp')
- grad_up_bias: float32 [4096], P('fsdp')
- grad_down_weight: float32 [4096, 1024], P('fsdp')
- grad_down_bias: float32 [1024], P('fsdp')
Inputs may be any that keep to these rules, and one draw needn't show every extreme that they name: qkv_weight has entries of order 1024^-0.5 times a few; its draw is a scaled normal law.
All inputs are finite; a program needn't handle non-finite values.
Results may differ from a plain program's by a relative error of at most 0.017.
Values may be sent and summed in bfloat16 or wider, within the bound.
A program may use at most 192 MiB of HBM per device.

v0:
```python
import math

import jax
import jax.numpy as jnp
from jax import lax
from jax.sharding import PartitionSpec as P

H = 16
ROT = 16
SEQ = 128


EPSILON = 1e-05
THETA = 10000.0
SQRT_HALF = 0.7071067811865476
INV_ROOT_TAU = 0.3989422804014327


def product(pattern, left_side, right_side):
    return jnp.einsum(pattern, left_side, right_side, preferred_element_type=jnp.float32)


def normalize(residual, gain_row, shift_row):
    centered = residual - jnp.mean(residual, axis=-1, keepdims=True)
    inverse = lax.rsqrt(jnp.mean(centered * centered, axis=-1, keepdims=True) + EPSILON)
    unit_rows = centered * inverse
    return (unit_rows * gain_row + shift_row, unit_rows, inverse)


def normalize_back(upstream, unit_rows, inverse, gain_row):
    scaled = upstream * gain_row
    grad_rows = inverse * (
        scaled
        - jnp.mean(scaled, axis=-1, keepdims=True)
        - unit_rows * jnp.mean(scaled * unit_rows, axis=-1, keepdims=True)
    )
    return (grad_rows, jnp.sum(upstream * unit_rows, axis=0), jnp.sum(upstream, axis=0))


def rotary_tables():
    half_rot = ROT // 2
    frequency = jnp.exp(jnp.arange(half_rot, dtype=jnp.float32) * (-2.0 * math.log(THETA) / ROT))
    angles = jnp.arange(SEQ, dtype=jnp.float32)[:, None] * frequency[None, :]
    return (jnp.cos(angles), jnp.sin(angles))


def rotate(heads_data, cosine_table, sine_table, inverse_turn):
    half_rot = ROT // 2
    first_half = heads_data[..., :half_rot]
    second_half = heads_data[..., half_rot:ROT]
    passive = heads_data[..., ROT:]
    cosine_part = cosine_table[None, :, None, :]
    sine_part = sine_table[None, :, None, :]
    if inverse_turn:
        sine_part = -sine_part
    return jnp.concatenate(
        [
            first_half * cosine_part - second_half * sine_part,
            second_half * cosine_part + first_half * sine_part,
            passive,
        ],
        axis=-1,
    )


def gelu_slope(pre_act):
    return (
        0.5 * (1.0 + lax.erf(pre_act * SQRT_HALF))
        + pre_act * jnp.exp(-0.5 * pre_act * pre_act) * INV_ROOT_TAU
    )


def masked_scores(queries, keys_rot):
    head_dim = queries.shape[-1]
    scores = product("bqhd,bkhd->bhqk", queries, keys_rot) * head_dim ** (-0.5)
    positions = jnp.arange(SEQ)
    causal = positions[:, None] >= positions[None, :]
    return jnp.where(causal[None, None], scores, -jnp.inf)


def forward_pass(inputs, forward_set):
    (
        attn_gain,
        attn_shift,
        qkv_weight,
        qkv_bias,
        proj_weight,
        proj_bias,
        mlp_gain,
        mlp_shift,
        up_weight,
        up_bias,
        down_weight,
        down_bias,
    ) = forward_set
    row_count, features = inputs.shape
    seq_count = row_count // SEQ
    head_dim = features // H
    residual = inputs.astype(jnp.float32)
    normed, attn_unit, attn_inverse = normalize(
        residual, attn_gain.astype(jnp.float32), attn_shift.astype(jnp.float32)
    )
    attn_in = normed.astype(jnp.bfloat16)
    projected = jnp.dot(attn_in, qkv_weight, preferred_element_type=jnp.float32) + qkv_bias.astype(
        jnp.float32
    )
    shaped = projected.reshape(seq_count, SEQ, 3, H, head_dim)
    cosine_table, sine_table = rotary_tables()
    queries = rotate(shaped[:, :, 0], cosine_table, sine_table, False).astype(jnp.bfloat16)
    keys_rot = rotate(shaped[:, :, 1], cosine_table, sine_table, False).astype(jnp.bfloat16)
    values = shaped[:, :, 2].astype(jnp.bfloat16)
    scores = masked_scores(queries, keys_rot)
    peak_score = jnp.max(scores, axis=-1, keepdims=True)
    logsum = peak_score + jnp.log(jnp.sum(jnp.exp(scores - peak_score), axis=-1, keepdims=True))
    weights = jnp.exp(scores - logsum).astype(jnp.bfloat16)
    context = (
        product("bhqk,bkhd->bqhd", weights, values)
        .reshape(row_count, features)
        .astype(jnp.bfloat16)
    )
    attn_out = jnp.dot(context, proj_weight, preferred_element_type=jnp.float32) + proj_bias.astype(
        jnp.float32
    )
    normed_mlp, mlp_unit, mlp_inverse = normalize(
        residual, mlp_gain.astype(jnp.float32), mlp_shift.astype(jnp.float32)
    )
    mlp_in = normed_mlp.astype(jnp.bfloat16)
    pre_act = jnp.dot(mlp_in, up_weight, preferred_element_type=jnp.float32) + up_bias.astype(
        jnp.float32
    )
    activated = jax.nn.gelu(pre_act, approximate=False).astype(jnp.bfloat16)
    mlp_out = jnp.dot(
        activated, down_weight, preferred_element_type=jnp.float32
    ) + down_bias.astype(jnp.float32)
    output = (residual + attn_out + mlp_out).astype(jnp.bfloat16)
    saved = (
        attn_unit,
        attn_inverse,
        attn_in,
        queries,
        keys_rot,
        values,
        logsum,
        context,
        mlp_unit,
        mlp_inverse,
        mlp_in,
        pre_act,
        activated,
    )
    return (output, saved)


def backward_pass(cotangent, saved, backward_set):
    (
        attn_gain,
        attn_shift,
        qkv_weight,
        qkv_bias,
        proj_weight,
        proj_bias,
        mlp_gain,
        mlp_shift,
        up_weight,
        up_bias,
        down_weight,
        down_bias,
    ) = backward_set
    (
        attn_unit,
        attn_inverse,
        attn_in,
        queries,
        keys_rot,
        values,
        logsum,
        context,
        mlp_unit,
        mlp_inverse,
        mlp_in,
        pre_act,
        activated,
    ) = saved
    row_count, features = cotangent.shape
    head_dim = features // H
    upstream = cotangent.astype(jnp.float32)
    grad_out_bias = jnp.sum(upstream, axis=0)
    grad_down_weight = jnp.dot(activated.T, cotangent, preferred_element_type=jnp.float32)
    grad_pre = jnp.dot(cotangent, down_weight.T, preferred_element_type=jnp.float32) * gelu_slope(
        pre_act
    )
    grad_up_bias = jnp.sum(grad_pre, axis=0)
    grad_pre_b = grad_pre.astype(jnp.bfloat16)
    grad_up_weight = jnp.dot(mlp_in.T, grad_pre_b, preferred_element_type=jnp.float32)
    grad_mlp_in = jnp.dot(grad_pre_b, up_weight.T, preferred_element_type=jnp.float32)
    grad_proj_weight = jnp.dot(context.T, cotangent, preferred_element_type=jnp.float32)
    grad_context = jnp.dot(cotangent, proj_weight.T, preferred_element_type=jnp.float32).astype(
        jnp.bfloat16
    )
    grad_context = grad_context.reshape(queries.shape)
    probs = jnp.exp(masked_scores(queries, keys_rot) - logsum)
    weights = probs.astype(jnp.bfloat16)
    grad_probs = product("bqhd,bkhd->bhqk", grad_context, values)
    grad_values = product("bhqk,bqhd->bkhd", weights, grad_context)
    grad_scores = (
        probs
        * (grad_probs - jnp.sum(probs * grad_probs, axis=-1, keepdims=True))
        * head_dim ** (-0.5)
    ).astype(jnp.bfloat16)
    grad_queries = product("bhqk,bkhd->bqhd", grad_scores, keys_rot)
    grad_keys = product("bhqk,bqhd->bkhd", grad_scores, queries)
    cosine_table, sine_table = rotary_tables()
    grad_projected = jnp.stack(
        [
            rotate(grad_queries, cosine_table, sine_table, True),
            rotate(grad_keys, cosine_table, sine_table, True),
            grad_values,
        ],
        axis=2,
    ).reshape(row_count, 3 * features)
    grad_qkv_bias = jnp.sum(grad_projected, axis=0)
    grad_projected_b = grad_projected.astype(jnp.bfloat16)
    grad_qkv_weight = jnp.dot(attn_in.T, grad_projected_b, preferred_element_type=jnp.float32)
    grad_attn_in = jnp.dot(grad_projected_b, qkv_weight.T, preferred_element_type=jnp.float32)
    attn_rows, grad_attn_gain, grad_attn_shift = normalize_back(
        grad_attn_in, attn_unit, attn_inverse, attn_gain.astype(jnp.float32)
    )
    mlp_rows, grad_mlp_gain, grad_mlp_shift = normalize_back(
        grad_mlp_in, mlp_unit, mlp_inverse, mlp_gain.astype(jnp.float32)
    )
    grad_inputs = (upstream + attn_rows + mlp_rows).astype(jnp.bfloat16)
    gradients = (
        grad_attn_gain,
        grad_attn_shift,
        grad_qkv_weight,
        grad_qkv_bias,
        grad_proj_weight,
        grad_out_bias,
        grad_mlp_gain,
        grad_mlp_shift,
        grad_up_weight,
        grad_up_bias,
        grad_down_weight,
        grad_out_bias,
    )
    return (grad_inputs, gradients)


def local(
    inputs,
    cotangent,
    attn_gain,
    attn_shift,
    qkv_weight,
    qkv_bias,
    proj_weight,
    proj_bias,
    mlp_gain,
    mlp_shift,
    up_weight,
    up_bias,
    down_weight,
    down_bias,
):
    attn_full = (
        lax.all_gather(attn_gain, "fsdp", axis=0, tiled=True),
        lax.all_gather(attn_shift, "fsdp", axis=0, tiled=True),
        lax.all_gather(qkv_weight, "fsdp", axis=0, tiled=True),
        lax.all_gather(qkv_bias, "fsdp", axis=0, tiled=True),
        lax.all_gather(proj_weight, "fsdp", axis=0, tiled=True),
        lax.all_gather(proj_bias, "fsdp", axis=0, tiled=True),
    )
    mlp_full = (
        lax.all_gather(mlp_gain, "fsdp", axis=0, tiled=True),
        lax.all_gather(mlp_shift, "fsdp", axis=0, tiled=True),
        lax.all_gather(up_weight, "fsdp", axis=0, tiled=True),
        lax.all_gather(up_bias, "fsdp", axis=0, tiled=True),
        lax.all_gather(down_weight, "fsdp", axis=0, tiled=True),
        lax.all_gather(down_bias, "fsdp", axis=0, tiled=True),
    )
    forward_set = tuple(attn_full) + tuple(mlp_full)
    output, saved = forward_pass(inputs, forward_set)
    grad_inputs, gradients = backward_pass(cotangent, saved, forward_set)
    attn_owned = (
        lax.psum_scatter(
            gradients[0].astype(jnp.bfloat16), "fsdp", scatter_dimension=0, tiled=True
        ).astype(jnp.float32),
        lax.psum_scatter(
            gradients[1].astype(jnp.bfloat16), "fsdp", scatter_dimension=0, tiled=True
        ).astype(jnp.float32),
        lax.psum_scatter(
            gradients[2].astype(jnp.bfloat16), "fsdp", scatter_dimension=0, tiled=True
        ).astype(jnp.float32),
        lax.psum_scatter(
            gradients[3].astype(jnp.bfloat16), "fsdp", scatter_dimension=0, tiled=True
        ).astype(jnp.float32),
        lax.psum_scatter(
            gradients[4].astype(jnp.bfloat16), "fsdp", scatter_dimension=0, tiled=True
        ).astype(jnp.float32),
        lax.psum_scatter(
            gradients[5].astype(jnp.bfloat16), "fsdp", scatter_dimension=0, tiled=True
        ).astype(jnp.float32),
    )
    mlp_owned = (
        lax.psum_scatter(gradients[6], "fsdp", scatter_dimension=0, tiled=True),
        lax.psum_scatter(gradients[7], "fsdp", scatter_dimension=0, tiled=True),
        lax.psum_scatter(gradients[8], "fsdp", scatter_dimension=0, tiled=True),
        lax.psum_scatter(gradients[9], "fsdp", scatter_dimension=0, tiled=True),
        lax.psum_scatter(gradients[10], "fsdp", scatter_dimension=0, tiled=True),
        lax.psum_scatter(gradients[11], "fsdp", scatter_dimension=0, tiled=True),
    )
    totals = lax.psum(
        (
            attn_owned[0],
            attn_owned[1],
            attn_owned[2],
            attn_owned[3],
            attn_owned[4],
            attn_owned[5],
            mlp_owned[0],
            mlp_owned[1],
            mlp_owned[2],
            mlp_owned[3],
            mlp_owned[4],
            mlp_owned[5],
        ),
        "replica",
    )
    return (
        output,
        grad_inputs,
        totals[0],
        totals[1],
        totals[2],
        totals[3],
        totals[4],
        totals[5],
        totals[6],
        totals[7],
        totals[8],
        totals[9],
        totals[10],
        totals[11],
    )


def solution(mesh):
    return jax.shard_map(
        local,
        mesh=mesh,
        in_specs=(
            P(("fsdp", "replica"), None),
            P(("fsdp", "replica"), None),
            P("fsdp"),
            P("fsdp"),
            P("fsdp", None),
            P("fsdp"),
            P("fsdp", None),
            P("fsdp"),
            P("fsdp"),
            P("fsdp"),
            P("fsdp", None),
            P("fsdp"),
            P("fsdp", None),
            P("fsdp"),
        ),
        out_specs=(
            P(("fsdp", "replica"), None),
            P(("fsdp", "replica"), None),
            P("fsdp"),
            P("fsdp"),
            P("fsdp", None),
            P("fsdp"),
            P("fsdp", None),
            P("fsdp"),
            P("fsdp"),
            P("fsdp"),
            P("fsdp", None),
            P("fsdp"),
            P("fsdp", None),
            P("fsdp"),
        ),
        check_vma=False,
    )
```

profile of v0, /device:TPU:0, one launch (start us, length us, event | category | flops | bytes accessed | tf_op | source)
XLA Modules:
  0.0 1370.3 jit_solution(6579028197176372335)
XLA Ops:
  7.2 0.7 all-gather.10.cloned.1.call-update
  8.0 0.7 all-gather.12.cloned.1.call-update
  8.7 0.7 all-gather.6.cloned.1.call-update
  9.5 0.5 all-gather.8.cloned.1.call-update
  10.0 0.7 reshape.296
  10.7 43.1 %all-gather = bf16[16,1,256]{2,1,0:T(2,128)(2,1)S(1)} all-gather(bf16[1,1,256]{2,1,0:T(2,128)(2,1)S(1)} %reshape.296), channel_id=1, replica_groups=mesh['fsdp'=16,'replica'=2] {'fsdp'}, dimensions={0}, use_global_device_ids=true | all-gather | bytes 8704 | tf_op jit(solution)/shard_map/all_gather | solution.py:277
  53.8 1.3 fusion.92
  56.5 0.8 dynamic-update-slice.5
  57.3 0.8 dynamic-update-slice.4
  58.2 0.8 dynamic-update-slice.1
  59.0 0.8 dynamic-update-slice
  59.8 0.8 dynamic-update-slice.2
  60.7 75.0 %all-reduce.19 = (bf16[1024]{0:T(1024)(128)(2,1)S(1)}, bf16[1024]{0:T(1024)(128)(2,1)S(1)}, bf16[3072]{0:T(1024)(128)(2,1)S(1)}, bf16[1024]{0:T(1024)(128)(2,1)S(1)}, bf16[1024]{0:T(1024)(128)(2,1)S(1)}) all-reduce(bf16[1024]{0:T(1024)(128)(2,1)S(1)} %dynamic-update-slice.5, ...), channel_id=1, replica_groups=mesh['fsdp'=16,'replica'=2] {'fsdp'}, use_global_device_ids=true, to_apply=%add.5 | all-reduce | flops 7168 | bytes 28672
  135.7 1.1 convert_reduce_fusion
  136.8 0.2 fusion.55
  137.0 9.4 fusion.3
  146.4 94.9 %all-gather.12.cloned.1.call-done = bf16[4096,1024]{1,0:T(8,128)(2,1)} async-done(((bf16[256,1024]{1,0:T(8,128)(2,1)}), bf16[4096,1024]{1,0:T(8,128)(2,1)}) %all-gather.12.cloned.1.call-update) | async-done | bytes 8388624 | tf_op jit(solution)/shard_map/all_gather | solution.py:278
  241.3 7.7 fusion.94
  248.9 1.0 copy-done.10
  249.9 8.2 fusion.56
  258.1 0.2 reduce-scatter.11.cloned.1.call-start
  258.4 8.1 fusion.95
  266.6 0.6 iota_compare_fusion
  267.2 0.1 fusion.80
  267.3 68.3 %all-gather.6.cloned.1.call-done = bf16[1024,3072]{1,0:T(8,128)(2,1)} async-done(((bf16[64,3072]{1,0:T(8,128)(2,1)}), bf16[1024,3072]{1,0:T(8,128)(2,1)}) %all-gather.6.cloned.1.call-update) | async-done | bytes 6291472 | tf_op jit(solution)/shard_map/all_gather | solution.py:268
  335.6 3.9 convolution_add_fusion.1
  339.5 0.5 copy.43
  340.2 0.5 copy-done.23
  340.7 0.4 fusion.93
  341.1 0.2 exponential_reduce_fusion
  341.3 0.3 convolution_convert_fusion.3
  341.6 0.7 copy-done.15
  342.3 2.0 convolution_convert_fusion.1
  344.4 52.9 %all-gather.8.cloned.1.call-done = bf16[1024,1024]{1,0:T(8,128)(2,1)} async-done(((bf16[64,1024]{1,0:T(8,128)(2,1)}), bf16[1024,1024]{1,0:T(8,128)(2,1)}) %all-gather.8.cloned.1.call-update) | async-done | bytes 2097168 | tf_op jit(solution)/shard_map/all_gather | solution.py:270
  397.2 2.4 convolution_convert_fusion.2
  399.6 0.2 copy.45
  399.8 1.4 fusion.71
  401.2 2.2 convolution_bitcast_fusion.1
  403.4 2.6 convolution_bitcast_fusion.2
  406.2 0.8 copy-done.14
  406.9 0.5 convolution_bitcast_fusion
  407.4 0.1 fusion.24
  407.6 0.2 copy-done.6
  407.8 0.9 copy-done.11
  408.6 4.6 convolution_convert_fusion
  413.2 0.3 all-reduce.23.cloned.1.call-start
  415.5 0.2 dynamic-update-slice.6
  415.7 0.2 dynamic-update-slice.3
  415.9 1.7 fusion.23
  417.6 0.1 convert_element_type.170
  417.7 6.8 fusion.58
  424.6 2.5 fusion.53
  427.1 317.5 %reduce-scatter.9.cloned.1.call-done = f32[64,4096]{1,0:T(8,128)} async-done(((f32[1024,4096]{1,0:T(8,128)}), f32[64,4096]{1,0:T(8,128)}) %reduce-scatter.9.cloned.1.call-update) | async-done | bytes 1048592 | tf_op jit(solution)/shard_map/reduce_scatter | solution.py:307
  744.6 354.2 %reduce-scatter.11.cloned.1.call-done = f32[256,1024]{1,0:T(8,128)} async-done(((f32[4096,1024]{1,0:T(8,128)}), f32[256,1024]{1,0:T(8,128)}) %reduce-scatter.11.cloned.1.call-update) | async-done | bytes 1048592 | tf_op jit(solution)/shard_map/reduce_scatter | solution.py:309
  1098.9 1.1 fusion.52
  1100.0 79.6 %all-reduce.18 = (bf16[1024]{0:T(1024)(128)(2,1)S(1)}, bf16[1024]{0:T(1024)(128)(2,1)S(1)}, bf16[1024]{0:T(1024)(128)(2,1)S(1)}, bf16[1024]{0:T(1024)(128)(2,1)S...) all-reduce(bf16[1024]{0:T(1024)(128)(2,1)S(1)} %dynamic-update-slic, ...), channel_id=1, replica_groups=mesh['fsdp'=16,'replica'=2] {'fsdp'}, use_global_device_ids=true, to_apply=%add.6 | all-reduce | flops 8192 | bytes 32768
  1179.6 72.4 %all-reduce.15 = (f32[1024]{0:T(1024)S(1)}, f32[1024]{0:T(1024)S(1)}, f32[4096]{0:T(1024)S(1)}, f32[1024]{0:T(1024)S(1)}) all-reduce(f32[1024]{0:T(1024)S(1)} %get-tuple-element.25, f32[1024]{0:T(1024)S(1)} %get-tuple-element.22, f32[4096]{0:T(1024)S(1)} %copy-done.22, ...), channel_id=8, replica_groups=mesh['fsdp'=16,'replica'=2] {'fsdp'}, use_global_device_ids=true, to_apply=%region_26.27.clone | all-reduce | flops 7168 | bytes 57344
  1252.6 4.8 convolution_add_fusion.3
  1257.5 1.2 fusion.22
  1258.7 78.9 %reduce-scatter.5.cloned.1.call-done = bf16[64,3072]{1,0:T(8,128)(2,1)} async-done(((bf16[1024,3072]{1,0:T(8,128)(2,1)}), bf16[64,3072]{1,0:T(8,128)(2,1)}) %reduce-scatter.5.cloned.1.call-update) | async-done | bytes 393232 | tf_op jit(solution)/shard_map/reduce_scatter | solution.py:291
  1337.5 7.3 all-reduce.24
  1344.9 15.6 %all-reduce.23.cloned.1.call-done = (f32[64,4096]{1,0:T(8,128)}, f32[256,1024]{1,0:T(8,128)}) async-done(((f32[64,4096]{1,0:T(8,128)}, f32[256,1024]{1,0:T(8,128)}), (f32[64,4096]{1,0:T(8,128)}, f32[256,1024]{1,0:T(8,128)})) %all-reduce.23.cloned.1.call-update) | async-done | bytes 2097168 | tf_op jit(solution)/shard_map/psum | solution.py:312
  1360.4 2.4 copy.74
  1362.8 1.0 copy.75
  (105 shorter events, 1.5 us)
Async XLA Ops:
  7.2 129.6 %copy-start = (bf16[128,1024]{1,0:T(8,128)(2,1)S(1)}, bf16[128,1024]{1,0:T(8,128)(2,1)}, u32[]{:S(2)}) copy-start(bf16[128,1024]{1,0:T(8,128)(2,1)} %param.14) | copy-start | bytes 786436
  7.2 129.8 %all-gather.10.cloned.1.call-start = ((), (), s32[]{:S(2)}) async-start(), calls=%async_computation.6 | async-start | bytes 8912896 | tf_op jit(solution)/shard_map/all_gather | solution.py:276
  7.9 233.3 %all-gather.12.cloned.1.call-start = ((), (), s32[]{:S(2)}) async-start(), calls=%async_computation.7 | async-start | bytes 8912896 | tf_op jit(solution)/shard_map/all_gather | solution.py:278
  8.7 327.0 %all-gather.6.cloned.1.call-start = ((), (), s32[]{:S(2)}) async-start(), calls=%async_computation.4 | async-start | bytes 6684672 | tf_op jit(solution)/shard_map/all_gather | solution.py:268
  9.4 387.8 %all-gather.8.cloned.1.call-start = ((), (), s32[]{:S(2)}) async-start(), calls=%async_computation.5 | async-start | bytes 2228224 | tf_op jit(solution)/shard_map/all_gather | solution.py:270
  10.0 734.6 %reduce-scatter.9.cloned.1.call-start = ((), (), s32[]{:S(2)}) async-start(), calls=%async_computation.10 | async-start | bytes 17825792 | tf_op jit(solution)/shard_map/reduce_scatter | solution.py:307
  137.0 104.2 %copy-start.7 = (bf16[128,1024]{1,0:T(8,128)(2,1)S(1)}, bf16[128,1024]{1,0:T(8,128)(2,1)}, u32[]{:S(2)}) copy-start(bf16[128,1024]{1,0:T(8,128)(2,1)} %param.15) | copy-start | bytes 786436
  146.4 111.9 %copy-start.2 = (bf16[128,4096]{1,0:T(8,128)(2,1)}, bf16[128,4096]{1,0:T(8,128)(2,1)S(1)}, u32[]{:S(2)}) copy-start(bf16[128,4096]{1,0:T(8,128)(2,1)S(1)} %get-tuple-element.74) | copy-start | bytes 3145732
  248.9 1.0 copy-start.10
  258.1 840.7 %reduce-scatter.11.cloned.1.call-start = ((), (), s32[]{:S(2)}) async-start(), calls=%async_computation.11 | async-start | bytes 17825792 | tf_op jit(solution)/shard_map/reduce_scatter | solution.py:309
  266.5 992.2 %reduce-scatter.7.cloned.1.call-start = ((), (), s32[]{:S(2)}) async-start(), calls=%async_computation.9 | async-start | bytes 2228224 | tf_op jit(solution)/shard_map/reduce_scatter | solution.py:297
  340.0 0.7 copy-start.23
  340.1 1.0 copy-start.21
  340.2 1.4 copy-start.18
  340.2 1.4 copy-start.20
  340.7 1.6 copy-start.8
  341.6 0.7 copy-start.15
  344.3 993.2 %reduce-scatter.5.cloned.1.call-start = ((), (), s32[]{:S(2)}) async-start(), calls=%async_computation.8 | async-start | bytes 6684672 | tf_op jit(solution)/shard_map/reduce_scatter | solution.py:291
  399.8 3.5 copy-start.13
  401.2 2.2 copy-start.19
  406.0 1.0 copy-start.14
  406.1 1.4 copy-start.4
  406.9 0.8 copy-start.6
  407.8 0.9 copy-start.11
  413.2 2.3 copy-start.24
  413.2 2.5 copy-start.25
  413.2 2.7 copy-start.5
  413.2 947.2 %all-reduce.23.cloned.1.call-start = ((), (), s32[]{:S(2)}) async-start(), calls=%async_computation.12 | async-start | bytes 4194304 | tf_op jit(solution)/shard_map/psum | solution.py:312
  415.9 8.6 slice-start
  417.7 6.9 slice-start.1
  417.7 6.9 copy-start.12
  427.1 671.8 %copy-start.9 = (bf16[128,1024]{1,0:T(8,128)(2,1)S(1)}, bf16[128,1024]{1,0:T(8,128)(2,1)}, u32[]{:S(2)}) copy-start(bf16[128,1024]{1,0:T(8,128)(2,1)} %param.15) | copy-start | bytes 786436
  427.1 752.5 %copy-start.22 = (f32[4096]{0:T(1024)S(1)}, f32[4096]{0:T(1024)}, u32[]{:S(2)}) copy-start(f32[4096]{0:T(1024)} %get-tuple-element.79) | copy-start | bytes 49156
  427.1 825.5 %copy-start.3 = (bf16[128,4096]{1,0:T(8,128)(2,1)S(1)}, bf16[128,4096]{1,0:T(8,128)(2,1)}, u32[]{:S(2)}) copy-start(bf16[128,4096]{1,0:T(8,128)(2,1)} %copy-done.2) | copy-start | bytes 3145732
  1252.6 4.9 copy-start.1
  1252.6 4.9 copy-start.16
  1360.4 2.4 copy-start.17
Sparse Core Ops, SparseCore 0:
  10.8 116.5 all-gather.9
  130.2 111.0 all-gather.11
  244.0 91.5 all-gather.5
  338.3 58.9 all-gather.7
  399.3 345.2 reduce-scatter.8
  746.8 352.0 reduce-scatter.10
  1101.1 87.1 reduce-scatter.6
  1193.5 143.9 reduce-scatter.4
  1339.9 20.4 all-reduce.22
where the time goes:
time: 1370 us
  waiting for transfers between devices  985 us (72%)
  blocking collectives  277 us (20%)
  matrix products  68.7 us (5%)
  between operations  17.6 us (1%)
  local copies, waits for them, and re-layouts  15.3 us (1%)
    reduce_scatter x1, waiting for transfers between devices, local(): lax.psum_scatter(gradients[10], 'fsdp', scatter_dimension=0, tiled=True)  354 us
    reduce_scatter x1, waiting for transfers between devices, local(): lax.psum_scatter(gradients[8], 'fsdp', scatter_dimension=0, tiled=True)  317 us
    unnamed x3, blocking collectives  227 us
    all_gather x1, waiting for transfers between devices, local(): lax.all_gather(down_weight, 'fsdp', axis=0, tiled=True)  94.9 us
    reduce_scatter x1, waiting for transfers between devices, local(): lax.psum_scatter(gradients[2].astype(jnp.bfloat16), 'fsdp', scatter_dimen...  78.9 us
    all_gather x1, waiting for transfers between devices, local(): lax.all_gather(qkv_weight, 'fsdp', axis=0, tiled=True)  68.3 us
    all_gather x1, waiting for transfers between devices, local(): lax.all_gather(proj_weight, 'fsdp', axis=0, tiled=True)  52.9 us
    all_gather x1, blocking collectives, local(): lax.all_gather(up_bias, 'fsdp', axis=0, tiled=True)  43.1 us
  transfers between devices with their start and end apart: 9, of which 7 were waited for; matrix products, arithmetic and copies ran while one was open for 6% of the time, Pallas kernels for 0%

commit v1 on v0

--- a/solution.py
+++ b/solution.py
@@ -76,6 +76,134 @@
     positions = jnp.arange(SEQ)
     causal = positions[:, None] >= positions[None, :]
     return jnp.where(causal[None, None], scores, -jnp.inf)
+
+
+ROW_TILE = 16
+
+
+def partner(x):
+    count = lax.axis_size("replica")
+    return lax.ppermute(x, "replica", [(i, i ^ 1) for i in range(count)])
+
+
+def parity():
+    return lax.rem(lax.axis_index("replica"), 2)
+
+
+def own_half(x):
+    half = x.shape[-1] // 2
+    return lax.dynamic_slice_in_dim(x, parity() * half, half, x.ndim - 1)
+
+
+def other_half(x):
+    half = x.shape[-1] // 2
+    return lax.dynamic_slice_in_dim(x, (1 - parity()) * half, half, x.ndim - 1)
+
+
+def pair_gather(rows):
+    return jnp.concatenate([rows, partner(rows)], axis=0)
+
+
+def pair_halves(rows):
+    return jnp.concatenate([own_half(rows), partner(other_half(rows))], axis=0)
+
+
+def fold(matrix, width):
+    return [matrix[:, k : k + width] for k in range(0, matrix.shape[1], width)]
+
+
+def apply_blocks(rows, blocks):
+    parts = [jnp.dot(rows, block, preferred_element_type=jnp.float32) for block in blocks]
+    return parts[0] if len(parts) == 1 else jnp.concatenate(parts, axis=-1)
+
+
+def apply_blocks_back(rows, blocks):
+    pieces = fold(rows, rows.shape[1] // len(blocks))
+    total = None
+    for piece, block in zip(pieces, blocks):
+        part = jnp.dot(piece, block.T, preferred_element_type=jnp.float32)
+        total = part if total is None else total + part
+    return total
+
+
+def pad_rows(flat, width):
+    tile = ROW_TILE * width
+    size = flat.shape[-1]
+    padded = -(-size // tile) * tile
+    widths = [(0, 0)] * (flat.ndim - 1) + [(0, padded - size)]
+    return jnp.pad(flat, widths).reshape(flat.shape[:-1] + (padded // width, width))
+
+
+def gather_all(matrices, vectors):
+    width = min(m.shape[1] for m in matrices)
+    packed = []
+    for matrix in matrices:
+        packed.extend(fold(matrix, width))
+    packed.append(pad_rows(jnp.concatenate(vectors), width))
+    full = lax.all_gather(jnp.concatenate(packed, axis=0), "fsdp", axis=0, tiled=False)
+    start = 0
+    whole = []
+    for matrix in matrices:
+        blocks = []
+        for _ in range(matrix.shape[1] // width):
+            blocks.append(full[:, start : start + matrix.shape[0]].reshape(-1, width))
+            start += matrix.shape[0]
+        whole.append(blocks)
+    tail = full[:, start:].reshape(full.shape[0], -1)
+    rows = []
+    start = 0
+    for vector in vectors:
+        rows.append(tail[:, start : start + vector.shape[0]].reshape(-1))
+        start += vector.shape[0]
+    return (whole, rows)
+
+
+def weight_grad(left_pair, right_pair, width):
+    return [
+        jnp.dot(left_pair.T, block, preferred_element_type=jnp.float32).astype(jnp.bfloat16)
+        for block in fold(right_pair, width)
+    ]
+
+
+def scatter_all(block_lists, vectors):
+    owners = lax.axis_size("fsdp")
+    width = block_lists[0][0].shape[1]
+    sums = jnp.concatenate([v.reshape(owners, -1) for v in vectors], axis=1)
+    sums = sums + partner(sums)
+    packed = [b.reshape(owners, -1, width) for blocks in block_lists for b in blocks]
+    packed.append(pad_rows(sums, width).astype(jnp.bfloat16))
+    owned = lax.psum_scatter(
+        jnp.concatenate(packed, axis=1), "fsdp", scatter_dimension=0, tiled=False
+    )
+    distance = 2
+    if distance < lax.axis_size("replica"):
+        owned = owned.astype(jnp.float32)
+    while distance < lax.axis_size("replica"):
+        count = lax.axis_size("replica")
+        moved = lax.ppermute(owned, "replica", [(i, i ^ distance) for i in range(count)])
+        owned = owned + moved
+        distance *= 2
+    main = sum(p.shape[1] for p in packed[:-1])
+    other = partner(owned[:main])
+    first = parity() == 0
+    left = jnp.where(first, owned[:main], other)
+    right = jnp.where(first, other, owned[:main])
+    start = 0
+    whole = []
+    for blocks in block_lists:
+        rows = blocks[0].shape[0] // owners
+        stop = start + rows * len(blocks)
+        pieces = [side[k : k + rows] for side in (left, right) for k in range(start, stop, rows)]
+        whole.append(jnp.concatenate(pieces, axis=1).astype(jnp.float32))
+        start = stop
+    tail = owned[main:].reshape(-1).astype(jnp.float32)
+    totals = []
+    start = 0
+    for vector in vectors:
+        size = vector.shape[0] // owners
+        totals.append(tail[start : start + size])
+        start += size
+    return (whole, totals)
 
 
 def forward_pass(inputs, forward_set):
@@ -101,7 +229,7 @@
         residual, attn_gain.astype(jnp.float32), attn_shift.astype(jnp.float32)
     )
     attn_in = normed.astype(jnp.bfloat16)
-    projected = jnp.dot(attn_in, qkv_weight, preferred_element_type=jnp.float32) + qkv_bias.astype(
+    projected = apply_blocks(attn_in, qkv_weight) + qkv_bias.astype(
         jnp.float32
     )
     shaped = projected.reshape(seq_count, SEQ, 3, H, head_dim)
@@ -118,20 +246,18 @@
         .reshape(row_count, features)
         .astype(jnp.bfloat16)
     )
-    attn_out = jnp.dot(context, proj_weight, preferred_element_type=jnp.float32) + proj_bias.astype(
+    attn_out = apply_blocks(context, proj_weight) + proj_bias.astype(
         jnp.float32
     )
     normed_mlp, mlp_unit, mlp_inverse = normalize(
         residual, mlp_gain.astype(jnp.float32), mlp_shift.astype(jnp.float32)
     )
     mlp_in = normed_mlp.astype(jnp.bfloat16)
-    pre_act = jnp.dot(mlp_in, up_weight, preferred_element_type=jnp.float32) + up_bias.astype(
+    pre_act = apply_blocks(mlp_in, up_weight) + up_bias.astype(
         jnp.float32
     )
     activated = jax.nn.gelu(pre_act, approximate=False).astype(jnp.bfloat16)
-    mlp_out = jnp.dot(
-        activated, down_weight, preferred_element_type=jnp.float32
-    ) + down_bias.astype(jnp.float32)
+    mlp_out = apply_blocks(activated, down_weight) + down_bias.astype(jnp.float32)
     output = (residual + attn_out + mlp_out).astype(jnp.bfloat16)
     saved = (
         attn_unit,
@@ -185,16 +311,18 @@
     head_dim = features // H
     upstream = cotangent.astype(jnp.float32)
     grad_out_bias = jnp.sum(upstream, axis=0)
-    grad_down_weight = jnp.dot(activated.T, cotangent, preferred_element_type=jnp.float32)
-    grad_pre = jnp.dot(cotangent, down_weight.T, preferred_element_type=jnp.float32) * gelu_slope(
+    cotangent_pair = pair_halves(cotangent)
+    half = features // 2
+    grad_down_weight = weight_grad(pair_gather(activated), cotangent_pair, half)
+    grad_pre = apply_blocks_back(cotangent, down_weight) * gelu_slope(
         pre_act
     )
     grad_up_bias = jnp.sum(grad_pre, axis=0)
     grad_pre_b = grad_pre.astype(jnp.bfloat16)
-    grad_up_weight = jnp.dot(mlp_in.T, grad_pre_b, preferred_element_type=jnp.float32)
-    grad_mlp_in = jnp.dot(grad_pre_b, up_weight.T, preferred_element_type=jnp.float32)
-    grad_proj_weight = jnp.dot(context.T, cotangent, preferred_element_type=jnp.float32)
-    grad_context = jnp.dot(cotangent, proj_weight.T, preferred_element_type=jnp.float32).astype(
+    grad_up_weight = weight_grad(pair_gather(mlp_in), pair_halves(grad_pre_b), half)
+    grad_mlp_in = apply_blocks_back(grad_pre_b, up_weight)
+    grad_proj_weight = weight_grad(pair_gather(context), cotangent_pair, half)
+    grad_context = apply_blocks_back(cotangent, proj_weight).astype(
         jnp.bfloat16
     )
     grad_context = grad_context.reshape(queries.shape)
@@ -220,8 +348,8 @@
     ).reshape(row_count, 3 * features)
     grad_qkv_bias = jnp.sum(grad_projected, axis=0)
     grad_projected_b = grad_projected.astype(jnp.bfloat16)
-    grad_qkv_weight = jnp.dot(attn_in.T, grad_projected_b, preferred_element_type=jnp.float32)
-    grad_attn_in = jnp.dot(grad_projected_b, qkv_weight.T, preferred_element_type=jnp.float32)
+    grad_qkv_weight = weight_grad(pair_gather(attn_in), pair_halves(grad_projected_b), half)
+    grad_attn_in = apply_blocks_back(grad_projected_b, qkv_weight)
     attn_rows, grad_attn_gain, grad_attn_shift = normalize_back(
         grad_attn_in, attn_unit, attn_inverse, attn_gain.astype(jnp.float32)
     )
@@ -262,69 +390,60 @@
     down_weight,
     down_bias,
 ):
-    attn_full = (
-        lax.all_gather(attn_gain, "fsdp", axis=0, tiled=True),
-        lax.all_gather(attn_shift, "fsdp", axis=0, tiled=True),
-        lax.all_gather(qkv_weight, "fsdp", axis=0, tiled=True),
-        lax.all_gather(qkv_bias, "fsdp", axis=0, tiled=True),
-        lax.all_gather(proj_weight, "fsdp", axis=0, tiled=True),
-        lax.all_gather(proj_bias, "fsdp", axis=0, tiled=True),
-    )
-    mlp_full = (
-        lax.all_gather(mlp_gain, "fsdp", axis=0, tiled=True),
-        lax.all_gather(mlp_shift, "fsdp", axis=0, tiled=True),
-        lax.all_gather(up_weight, "fsdp", axis=0, tiled=True),
-        lax.all_gather(up_bias, "fsdp", axis=0, tiled=True),
-        lax.all_gather(down_weight, "fsdp", axis=0, tiled=True),
-        lax.all_gather(down_bias, "fsdp", axis=0, tiled=True),
-    )
-    forward_set = tuple(attn_full) + tuple(mlp_full)
+    weights, vectors = gather_all(
+        (qkv_weight, proj_weight, up_weight, down_weight),
+        (
+            attn_gain,
+            attn_shift,
+            qkv_bias,
+            proj_bias,
+            mlp_gain,
+            mlp_shift,
+            up_bias,
+            down_bias,
+        ),
+    )
+    forward_set = (
+        vectors[0],
+        vectors[1],
+        weights[0],
+        vectors[2],
+        weights[1],
+        vectors[3],
+        vectors[4],
+        vectors[5],
+        weights[2],
+        vectors[6],
+        weights[3],
+        vectors[7],
+    )
     output, saved = forward_pass(inputs, forward_set)
     grad_inputs, gradients = backward_pass(cotangent, saved, forward_set)
-    attn_owned = (
-        lax.psum_scatter(
-            gradients[0].astype(jnp.bfloat16), "fsdp", scatter_dimension=0, tiled=True
-        ).astype(jnp.float32),
-        lax.psum_scatter(
-            gradients[1].astype(jnp.bfloat16), "fsdp", scatter_dimension=0, tiled=True
-        ).astype(jnp.float32),
-        lax.psum_scatter(
-            gradients[2].astype(jnp.bfloat16), "fsdp", scatter_dimension=0, tiled=True
-        ).astype(jnp.float32),
-        lax.psum_scatter(
-            gradients[3].astype(jnp.bfloat16), "fsdp", scatter_dimension=0, tiled=True
-        ).astype(jnp.float32),
-        lax.psum_scatter(
-            gradients[4].astype(jnp.bfloat16), "fsdp", scatter_dimension=0, tiled=True
-        ).astype(jnp.float32),
-        lax.psum_scatter(
-            gradients[5].astype(jnp.bfloat16), "fsdp", scatter_dimension=0, tiled=True
-        ).astype(jnp.float32),
-    )
-    mlp_owned = (
-        lax.psum_scatter(gradients[6], "fsdp", scatter_dimension=0, tiled=True),
-        lax.psum_scatter(gradients[7], "fsdp", scatter_dimension=0, tiled=True),
-        lax.psum_scatter(gradients[8], "fsdp", scatter_dimension=0, tiled=True),
-        lax.psum_scatter(gradients[9], "fsdp", scatter_dimension=0, tiled=True),
-        lax.psum_scatter(gradients[10], "fsdp", scatter_dimension=0, tiled=True),
-        lax.psum_scatter(gradients[11], "fsdp", scatter_dimension=0, tiled=True),
-    )
-    totals = lax.psum(
+    matrices, rows = scatter_all(
+        (gradients[2], gradients[4], gradients[8], gradients[10]),
         (
-            attn_owned[0],
-            attn_owned[1],
-            attn_owned[2],
-            attn_owned[3],
-            attn_owned[4],
-            attn_owned[5],
-            mlp_owned[0],
-            mlp_owned[1],
-            mlp_owned[2],
-            mlp_owned[3],
-            mlp_owned[4],
-            mlp_owned[5],
+            gradients[0],
+            gradients[1],
+            gradients[3],
+            gradients[5],
+            gradients[6],
+            gradients[7],
+            gradients[9],
         ),
-        "replica",
+    )
+    totals = (
+        rows[0],
+        rows[1],
+        matrices[0],
+        rows[2],
+        matrices[1],
+        rows[3],
+        rows[4],
+        rows[5],
+        matrices[2],
+        rows[6],
+        matrices[3],
+        rows[3],
     )
     return (
         output,

time: 1370 us -> 693 us (0.51)
  waiting for transfers between devices: 985 us -> 540 us
  blocking collectives: 277 us -> 0 us
  local copies, waits for them, and re-layouts: 15.3 us -> 64.2 us
  matrix products: 68.7 us -> 45.9 us
  other arithmetic: 5.64 us -> 20.3 us
    reduce_scatter x4 -> x1, waiting for transfers between devices: 751 us -> 265 us  [scatter_all(): lax.psum_scatter(jnp.concatenate(packed, axis=1), 'fsdp', scatter_dimensi...]
    unnamed x3 -> x0, blocking collectives: 227 us -> none
    all_gather x4 -> x1, waiting for transfers between devices: 216 us -> 275 us  [gather_all(): lax.all_gather(jnp.concatenate(packed, axis=0), 'fsdp', axis=0, tiled=False)]
    all_gather x1 -> x0, blocking collectives: 43.1 us -> none  [local(): lax.all_gather(up_bias, 'fsdp', axis=0, tiled=True)]
    dot_general x12 -> x27, matrix products: 61.5 us -> 34.2 us  [the longest x9 13.5 us: apply_blocks_back(): part = jnp.dot(piece, block.T, preferred_element_type=jnp.float32)]
    slice x0 -> x9, local copies, waits for them, and re-layouts: none -> 24.6 us  [the longest x2 19.7 us: gather_all(): blocks.append(full[:, start:start + matrix.shape[0]].reshape(-1, width))]
    psum x1 -> x0, waiting for transfers between devices: 15.6 us -> none  [local(): lax.psum((attn_owned[0], attn_owned[1], attn_owned[2], attn_owned[3], att...]
  transfers between devices with their start and end apart: 9 -> 11, of which waited for: 7 -> 2; matrix products, arithmetic and copies ran while one was open for 6% -> 14% of each run, Pallas kernels for 0% -> 0%
where the time goes in v1:
time: 693 us; the launch traced here: 688 us
  waiting for transfers between devices  540 us (78%)
  local copies, waits for them, and re-layouts  64.2 us (9%)
  matrix products  45.9 us (7%)
  other arithmetic  20.3 us (3%)
  between operations  15 us (2%)
    all_gather x1, waiting for transfers between devices, gather_all(): lax.all_gather(jnp.concatenate(packed, axis=0), 'fsdp', axis=0, tiled=False)  275 us
    reduce_scatter x1, waiting for transfers between devices, scatter_all(): lax.psum_scatter(jnp.concatenate(packed, axis=1), 'fsdp', scatter_dimensi...  265 us
    unnamed x114, local copies, waits for them, and re-layouts  26.5 us
    slice x2, local copies, waits for them, and re-layouts, gather_all(): blocks.append(full[:, start:start + matrix.shape[0]].reshape(-1, width))  19.7 us
  transfers between devices with their start and end apart: 11, of which 2 were waited for; matrix products, arithmetic and copies ran while one was open for 14% of the time, Pallas kernels for 0%

profile of v1, /device:TPU:0, one launch (start us, length us, event | category | flops | bytes accessed | tf_op | source)
XLA Modules:
  0.0 688.2 jit_solution(4664165163374241804)
XLA Ops:
  7.2 5.5 concatenate.87
  12.7 0.9 slice_dynamic-update-slice_fusion.6
  13.7 0.9 slice_dynamic-update-slice_fusion.5
  14.6 0.9 slice_dynamic-update-slice_fusion.4
  15.5 1.0 constant_dynamic-update-slice_fusion.2
  16.5 0.9 slice_dynamic-update-slice_fusion.3
  17.4 1.0 slice_dynamic-update-slice_fusion.2
  18.4 0.9 slice_dynamic-update-slice_fusion.1
  19.3 0.9 slice_dynamic-update-slice_fusion
  20.3 1.2 copy-done.21
  24.4 275.4 %all-gather.3.cloned.1.call-done = bf16[12544,1024]{1,0:T(8,128)(2,1)} async-done(((bf16[784,1024]{1,0:T(8,128)(2,1)}), bf16[12544,1024]{1,0:T(8,128)(2,1)}) %all-gather.3.cloned.1.call-update) | async-done | bytes 25690128 | tf_op jit(solution)/shard_map/all_gather | solution.py:143
  299.8 1.1 slice.334
  302.5 8.0 %slice.359 = bf16[16,256,1024]{2,1,0:T(8,128)(2,1)} slice(bf16[16,784,1024]{2,1,0:T(8,128)(2,1)} %bitcast.123), slice={[0:16], [512:768], [0:1024]} | slice | bytes 16777216 | tf_op jit(solution)/shard_map/slice | solution.py:149
  310.5 11.7 %fusion.121 = (bf16[16,64,1024]{2,1,0:T(8,128)(2,1)S(1)}, bf16[16,64,1024]{2,1,0:T(8,128)(2,1)}, bf16[16,64,1024]{2,1,0:T(8,128)(2,1)}, bf16[16,64,1024]{2,1,0:T...) fusion(bf16[16,784,1024]{2,1,0:T(8,128)(2,1)} %bitcast.124), kind=kLoop, calls=%fused_computation.249 | loop fusion | bytes 33554432 | tf_op jit(solution)/shard_map/slice | solution.py:149
  323.5 0.7 convolution_convert_fusion.9
  325.2 0.8 copy-done
  327.4 1.3 pad_maximum_fusion
  328.7 3.0 copy.33
  331.7 1.9 broadcast_add_fusion
  333.8 1.3 fusion.95
  335.8 0.8 copy-done.7
  336.6 1.0 convolution_convert_fusion.10
  337.6 3.5 convolution_bitcast_fusion.2
  341.1 3.6 convolution_bitcast_fusion.3
  344.7 1.9 convolution_bitcast_fusion.1
  346.9 1.1 fusion.27
  348.0 1.0 fusion.28
  350.5 1.3 copy-done.6
  352.3 5.3 fusion.4
  357.6 4.1 fusion.122
  361.7 0.8 fusion.85
  362.5 0.8 convolution_add_fusion.2
  363.3 0.8 convolution_add_fusion.1
  364.2 1.6 convolution_add_fusion
  365.9 2.6 fusion.89
  368.6 0.8 convolution_add_fusion.4
  369.5 0.7 copy-done.9
  370.3 1.1 fusion.57
  371.5 1.1 convert_reduce_fusion.1
  373.6 1.2 constant_dynamic-slice_fusion.4
  376.3 1.4 convolution_convert_fusion.5
  377.7 1.4 convolution_convert_fusion.8
  379.2 1.1 constant_dynamic-update-slice_fusion.12
  380.3 1.4 convolution_convert_fusion.7
  381.7 1.1 constant_dynamic-update-slice_fusion.11
  382.8 1.4 convolution_convert_fusion.6
  384.2 1.1 constant_dynamic-update-slice_fusion.10
  385.3 1.1 constant_dynamic-update-slice_fusion.9
  386.9 1.1 constant_dynamic-update-slice_fusion.8
  388.5 1.1 constant_dynamic-update-slice_fusion.7
  390.1 1.1 constant_dynamic-update-slice_fusion.6
  391.7 1.1 constant_dynamic-update-slice_fusion.5
  392.8 2.2 convolution_convert_fusion
  395.0 2.5 constant_dynamic-update-slice_fusion.4
  397.5 0.7 constant_dynamic-update-slice_fusion.3
  399.0 264.9 %reduce-scatter.2.cloned.1.call-done = bf16[1,784,512]{2,1,0:T(8,128)(2,1)} async-done(((bf16[16,784,512]{2,1,0:T(8,128)(2,1)}), bf16[1,784,512]{2,1,0:T(8,128)(2,1)}) %reduce-scatter.2.cloned.1.call-update) | async-done | bytes 802832 | tf_op jit(solution)/shard_map/reduce_scatter | solution.py:175
  663.9 2.1 slice_bitcast_fusion
  665.9 5.4 convolution_add_fusion.6
  671.5 2.4 fusion.26
  675.6 1.2 broadcast_select_fusion
  677.0 1.0 convert_element_type.262
  678.1 0.9 convert_element_type.260
  679.0 1.1 maximum_convert_fusion
  680.1 0.7 maximum_convert_fusion.1
  (183 shorter events, 18.8 us)
Async XLA Ops:
  7.2 13.0 %copy-start.24 = (bf16[256,1024]{1,0:T(8,128)(2,1)S(1)}, bf16[256,1024]{1,0:T(8,128)(2,1)}, u32[]{:S(2)}) copy-start(bf16[256,1024]{1,0:T(8,128)(2,1)} %param.26) | copy-start | bytes 1572868
  7.2 292.6 %all-gather.3.cloned.1.call-start = ((), (), s32[]{:S(2)}) async-start(), calls=%async_computation.2 | async-start | bytes 27295744 | tf_op jit(solution)/shard_map/all_gather | solution.py:143
  15.5 6.0 copy-start.18
  17.4 6.0 copy-start.12
  20.3 1.2 copy-start.21
  21.5 642.4 %reduce-scatter.2.cloned.1.call-start = ((), (), s32[]{:S(2)}) async-start(), calls=%async_computation.1 | async-start | bytes 13647872 | tf_op jit(solution)/shard_map/reduce_scatter | solution.py:175
  22.2 353.5 %collective-permute-start.3 = (bf16[128,512]{1,0:T(8,128)(2,1)}, bf16[128,512]{1,0:T(8,128)(2,1)}, u32[]{:S(2)}, u32[]{:S(2)}) collective-permute-start(bf16[128,512]{1,0:T(8,128)(2,1)} %get-tuple-element.77), channel_id=1, source_target_pairs={{0,1},{1,0},{2,3},{3,2},{4,5},{5,4},{6,7},{7,6},{8,9},{9,8},{10,11... | collective-permute-start | bytes 393224 | tf_op jit(solution)/shard_map/ppermute | solution.py:86
  23.5 299.7 %copy-start.35 = (f32[128]{0:T(128)}, f32[128]{0:T(128)S(1)}, u32[]{:S(2)}) copy-start(f32[128]{0:T(128)S(1)} %broadcast_multiply_fusion.4) | copy-start | bytes 1540
  23.7 299.5 %copy-start.37 = (f32[128]{0:T(128)}, f32[128]{0:T(128)S(1)}, u32[]{:S(2)}) copy-start(f32[128]{0:T(128)S(1)} %add_rsqrt_fusion) | copy-start | bytes 1540
  24.4 310.7 %copy-start.28 = (f32[128,8]{0,1:T(8,128)}, f32[128,8]{0,1:T(8,128)S(1)}, u32[]{:S(2)}) copy-start(f32[128,8]{0,1:T(8,128)S(1)} %get-tuple-element.89) | copy-start | bytes 12292
  323.2 1.6 copy-start.8
  323.4 54.3 %collective-permute-start = (bf16[128,1024]{1,0:T(8,128)(2,1)S(1)}, bf16[128,1024]{1,0:T(8,128)(2,1)}, u32[]{:S(2)}, u32[]{:S(2)}) collective-permute-start(bf16[128,1024]{1,0:T(8,128)(2,1)S(1)} %get-tuple-element.72), channel_id=1, source_target_pairs={{0,1},{1,0},{2,3},{3,2},{4,5},{5,4},{6,7},{7,6},{8,9},{9,8},{10,11... | collective-permute-start | bytes 786440 | tf_op jit(solution)/shard_map/ppermute | solution.py:86
  324.2 9.5 %copy-start.17 = (bf16[1024,128]{1,0:T(8,128)(2,1)}, bf16[1024,128]{1,0:T(8,128)(2,1)S(1)}, u32[]{:S(2)}) copy-start(bf16[1024,128]{1,0:T(8,128)(2,1)S(1)} %convolution_convert_fusion.9) | copy-start | bytes 786436
  324.2 1.8 copy-start
  325.2 1.7 copy-start.2
  328.7 3.0 copy-start.25
  333.6 1.6 copy-start.34
  335.2 0.6 copy-start.30
  335.6 1.0 copy-start.7
  344.7 1.9 copy-start.22
  344.7 1.9 copy-start.23
  344.7 2.0 copy-start.29
  344.7 2.0 copy-start.33
  344.7 2.0 slice-start.3
  344.7 2.1 slice-start.2
  346.8 2.2 copy-start.27
  346.9 2.1 copy-start.3
  346.9 2.6 copy-start.4
  346.9 3.1 copy-start.5
  348.0 9.6 %slice-start = ((s8[8388608]{0:T(1024)(128)(4,1)}), s8[4194304]{0:T(1024)(128)(4,1)S(1)}, s32[]{:S(2)}) async-start(s8[8388608]{0:T(1024)(128)(4,1)} %bitcast.119), calls=%async_computation.3 | async-start | bytes 8388608
  349.9 1.9 copy-start.6
  350.0 7.6 %slice-start.1 = ((s8[8388608]{0:T(1024)(128)(4,1)}), s8[4194304]{0:T(1024)(128)(4,1)S(1)}, s32[]{:S(2)}) async-start(s8[8388608]{0:T(1024)(128)(4,1)} %bitcast.119), calls=%async_computation.4 | async-start | bytes 8388608
  352.3 5.3 copy-start.19
  361.7 2.5 copy-start.14
  364.2 1.7 copy-start.26
  365.9 2.7 copy-start.1
  365.9 2.7 copy-start.13
  368.6 1.6 copy-start.9
  368.6 1.7 copy-start.20
  368.6 1.7 copy-start.36
  368.6 1.6 copy-start.38
  373.0 2.1 copy-start.15
  373.0 2.2 collective-permute-start.7
  373.2 2.8 copy-start.10
  373.2 2.7 collective-permute-start.2
  374.8 2.9 collective-permute-start.1
  375.2 11.2 %collective-permute-start.4 = (bf16[128,1024]{1,0:T(8,128)(2,1)S(1)}, bf16[128,1024]{1,0:T(8,128)(2,1)S(1)}, u32[]{:S(2)}, u32[]{:S(2)}) collective-permute-start(bf16[128,1024]{1,0:T(8,128)(2,1)S(1)} %get-tuple-element.73), channel_id=1, source_target_pairs={{0,1},{1,0},{2,3},{3,2},{4,5},{5,4},{6,7},{7,6},{8,9},{9,8},{10,11... | collective-permute-start | bytes 786440 | tf_op jit(solution)/shard_map/ppermute | solution.py:86
  375.7 10.7 %collective-permute-start.5 = (bf16[128,2048]{1,0:T(8,128)(2,1)S(1)}, bf16[128,2048]{1,0:T(8,128)(2,1)S(1)}, u32[]{:S(2)}, u32[]{:S(2)}) collective-permute-start(bf16[128,2048]{1,0:T(8,128)(2,1)S(1)} %get-tuple-element.40), channel_id=1, source_target_pairs={{0,1},{1,0},{2,3},{3,2},{4,5},{5,4},{6,7},{7,6},{8,9},{9,8},{10,11... | collective-permute-start | bytes 1572872 | tf_op jit(solution)/shard_map/ppermute | solution.py:86
  376.0 16.8 %collective-permute-start.6 = (bf16[128,4096]{1,0:T(8,128)(2,1)S(1)}, bf16[128,4096]{1,0:T(8,128)(2,1)S(1)}, u32[]{:S(2)}, u32[]{:S(2)}) collective-permute-start(bf16[128,4096]{1,0:T(8,128)(2,1)S(1)} %copy-done.10), channel_id=1, source_target_pairs={{0,1},{1,0},{2,3},{3,2},{4,5},{5,4},{6,7},{7,6},{8,9},{9,8},{10,11... | collective-permute-start | bytes 3145736 | tf_op jit(solution)/shard_map/ppermute | solution.py:86
  398.2 0.7 copy-start.32
  398.2 267.7 %copy-start.11 = (bf16[128,4096]{1,0:T(8,128)(2,1)S(1)}, bf16[128,4096]{1,0:T(8,128)(2,1)}, u32[]{:S(2)}) copy-start(bf16[128,4096]{1,0:T(8,128)(2,1)} %fusion.4) | copy-start | bytes 3145732
  665.9 5.5 copy-start.31
  665.9 9.6 %collective-permute-start.8 = (bf16[768,512]{1,0:T(8,128)(2,1)}, bf16[768,512]{1,0:T(8,128)(2,1)}, u32[]{:S(2)}, u32[]{:S(2)}) collective-permute-start(bf16[768,512]{1,0:T(8,128)(2,1)} %slice_bitcast_fusion), channel_id=1, source_target_pairs={{0,1},{1,0},{2,3},{3,2},{4,5},{5,4},{6,7},{7,6},{8,9},{9,8},{10,11... | collective-permute-start | bytes 2359304 | tf_op jit(solution)/shard_map/ppermute | solution.py:86
  671.4 2.4 copy-start.16
  675.6 5.2 copy-start.39
Sparse Core Ops, SparseCore 0:
  21.6 278.1 all-gather.2
  398.4 265.4 reduce-scatter.1
